TPU v7x, 32 devices: a whole 2x2x4 slice. The times are simulated.
32 devices in a mesh: groups: 2 (over y), row: 4 (over z), col: 4 (over x, core).
Axes of the slice: x: 2, y: 2, z: 4, core: 2. Of those that a mesh axis runs over, the one named last changes fastest.
Arguments:
- factor_blocks: bfloat16 [20, 4096, 4096], P('groups', 'row', 'col'), parts along dimension 0, may hold values from -0.0390625 to 0.0390625
- inverse_blocks: bfloat16 [10, 4096, 4096], P('groups', 'col', 'row'), parts along dimension 0, as said below
- right_sides: bfloat16 [10, 4096, 256], P('groups', 'row'), parts along dimension 0, may hold values from -6 to 6
Outputs:
- solution: bfloat16 [10, 4096, 256], P('groups', 'col', 'row'), parts along dimension 0
There are 2 independent parts, one for each index of `groups`. A program takes and returns all parts, laid end to end along the dimension named above; each array names one. Nothing has to cross between parts.
Inputs may be any that keep to these rules, and one draw needn't show every extreme that they name: `inverse_blocks`: each block is lower triangular with a diagonal of 0.5 to 2, hence invertible.
All inputs are finite; a program needn't handle non-finite values.
Results may differ from a plain program's by a relative error of at most 0.0095.
Values may be sent and summed in bfloat16 or wider, within the bound.
A program may use at most 64 MiB of HBM per device.

v0:
```python
import jax
import jax.numpy as jnp
from jax import lax
from jax.sharding import PartitionSpec as P


def pair_index(block_row, column_index):
    return block_row * (block_row - 1) // 2 + column_index


def per_device(factor_blocks, inverse_blocks, right_sides):
    steps_total = right_sides.shape[0]
    angles = right_sides.shape[2]
    col_rows = inverse_blocks.shape[1]
    solved = []
    outputs = []
    for block_row in range(steps_total):
        residual = right_sides[block_row].astype(jnp.float32)
        if block_row > 0:
            partial_value = jnp.zeros((right_sides.shape[1], angles), jnp.float32)
            for column_index in range(block_row):
                partial_value = partial_value + jnp.dot(
                    factor_blocks[pair_index(block_row, column_index)],
                    solved[column_index],
                    preferred_element_type=jnp.float32,
                )
            residual = residual - lax.psum(partial_value, "col")
        residual_bf = residual.astype(jnp.bfloat16)
        term = jnp.dot(inverse_blocks[block_row], residual_bf, preferred_element_type=jnp.float32)
        share = lax.psum_scatter(term, "row", scatter_dimension=1, tiled=True).astype(jnp.bfloat16)
        outputs.append(share)
        if block_row + 1 < steps_total:
            current = lax.all_gather(share, "row", axis=1, tiled=True)
        else:
            current = jnp.zeros((col_rows, angles), jnp.bfloat16)
        solved.append(current)
    return jnp.stack(outputs, axis=0)


def solution(mesh):
    placed = (P("groups", "row", "col"), P("groups", "col", "row"), P("groups", "row", None))
    return jax.shard_map(
        per_device, mesh=mesh, in_specs=placed, out_specs=P("groups", "col", "row"), check_vma=False
    )
```

profile of v0, /device:TPU:26, one launch (start us, length us, event | category | flops | bytes accessed | tf_op | source)
XLA Modules:
  0.0 402.4 jit_solution(15479284260959443623)
XLA Ops:
  6.5 3.4 fusion.28
  10.0 25.9 %reduce-scatter.6.cloned.1.call-done = f32[1024,64]{0,1:T(8,128)} async-done(((f32[1024,256]{0,1:T(8,128)}), f32[1024,64]{0,1:T(8,128)}) %reduce-scatter.6.cloned.1.call-update) | async-done | bytes 262160 | tf_op jit(solution)/shard_map/reduce_scatter | solution.py:30
  35.9 1.6 bitcast_dynamic-update-slice_fusion.4
  37.6 15.0 %all_gather.12 = bf16[1024,256]{0,1:T(8,128)(2,1)S(1)} all-gather(bf16[1024,64]{0,1:T(8,128)(2,1)S(1)} %get-tuple-element.12), channel_id=1, replica_groups=mesh['groups'=2,'row'=4,'col'=4] {'row'}, dimensions={1}, use_global_device_ids=true | all-gather | bytes 655360 | tf_op jit(solution)/shard_map/all_gather | solution.py:33
  52.6 3.5 fusion.45
  56.1 37.7 %all-reduce.5.cloned.1.call-done = f32[1024,256]{1,0:T(8,128)} async-done(((f32[1024,256]{1,0:T(8,128)}), f32[1024,256]{1,0:T(8,128)}) %all-reduce.5.cloned.1.call-update) | async-done | bytes 1048592 | tf_op jit(solution)/shard_map/psum | solution.py:27
  93.8 3.7 fusion.48
  97.6 25.9 %reduce-scatter.8.cloned.1.call-done = f32[1024,64]{0,1:T(8,128)} async-done(((f32[1024,256]{0,1:T(8,128)}), f32[1024,64]{0,1:T(8,128)}) %reduce-scatter.8.cloned.1.call-update) | async-done | bytes 262160 | tf_op jit(solution)/shard_map/reduce_scatter | solution.py:30
  123.4 1.6 bitcast_dynamic-update-slice_fusion.3
  125.1 14.9 %all_gather.13 = bf16[1024,256]{0,1:T(8,128)(2,1)S(1)} all-gather(bf16[1024,64]{0,1:T(8,128)(2,1)S(1)} %get-tuple-element.10), channel_id=1, replica_groups=mesh['groups'=2,'row'=4,'col'=4] {'row'}, dimensions={1}, use_global_device_ids=true | all-gather | bytes 655360 | tf_op jit(solution)/shard_map/all_gather | solution.py:33
  140.8 2.3 fusion.20
  143.1 3.3 fusion.63
  146.5 37.7 %all-reduce.7.cloned.1.call-done = f32[1024,256]{1,0:T(8,128)} async-done(((f32[1024,256]{1,0:T(8,128)}), f32[1024,256]{1,0:T(8,128)}) %all-reduce.7.cloned.1.call-update) | async-done | bytes 1048592 | tf_op jit(solution)/shard_map/psum | solution.py:27
  184.2 3.6 fusion.51
  188.0 3.5 fusion.14
  191.5 22.4 %reduce-scatter.10.cloned.1.call-done = f32[1024,64]{0,1:T(8,128)} async-done(((f32[1024,256]{0,1:T(8,128)}), f32[1024,64]{0,1:T(8,128)}) %reduce-scatter.10.cloned.1.call-update) | async-done | bytes 262160 | tf_op jit(solution)/shard_map/reduce_scatter | solution.py:30
  213.9 1.7 bitcast_dynamic-update-slice_fusion.2
  215.6 14.9 %all_gather.14 = bf16[1024,256]{0,1:T(8,128)(2,1)S(1)} all-gather(bf16[1024,64]{0,1:T(8,128)(2,1)S(1)} %get-tuple-element.8), channel_id=1, replica_groups=mesh['groups'=2,'row'=4,'col'=4] {'row'}, dimensions={1}, use_global_device_ids=true | all-gather | bytes 655360 | tf_op jit(solution)/shard_map/all_gather | solution.py:33
  231.3 2.3 fusion.12
  233.7 3.3 fusion.72
  237.1 37.7 %all-reduce.9.cloned.1.call-done = f32[1024,256]{1,0:T(8,128)} async-done(((f32[1024,256]{1,0:T(8,128)}), f32[1024,256]{1,0:T(8,128)}) %all-reduce.9.cloned.1.call-update) | async-done | bytes 1048592 | tf_op jit(solution)/shard_map/psum | solution.py:27
  274.8 3.6 fusion.54
  278.5 3.6 fusion.6
  282.1 3.3 fusion.4
  285.4 19.0 %reduce-scatter.12.cloned.1.call-done = f32[1024,64]{0,1:T(8,128)} async-done(((f32[1024,256]{0,1:T(8,128)}), f32[1024,64]{0,1:T(8,128)}) %reduce-scatter.12.cloned.1.call-update) | async-done | bytes 262160 | tf_op jit(solution)/shard_map/reduce_scatter | solution.py:30
  304.4 1.8 bitcast_dynamic-update-slice_fusion.1
  306.1 14.9 %all_gather.15 = bf16[1024,256]{0,1:T(8,128)(2,1)S(1)} all-gather(bf16[1024,64]{0,1:T(8,128)(2,1)S(1)} %get-tuple-element.6), channel_id=1, replica_groups=mesh['groups'=2,'row'=4,'col'=4] {'row'}, dimensions={1}, use_global_device_ids=true | all-gather | bytes 655360 | tf_op jit(solution)/shard_map/all_gather | solution.py:33
  321.1 2.3 fusion.2
  323.4 3.4 fusion.84
  326.9 37.7 %all-reduce.11.cloned.1.call-done = f32[1024,256]{1,0:T(8,128)} async-done(((f32[1024,256]{1,0:T(8,128)}), f32[1024,256]{1,0:T(8,128)}) %all-reduce.11.cloned.1.call-update) | async-done | bytes 1048592 | tf_op jit(solution)/shard_map/psum | solution.py:27
  364.6 3.7 fusion.57
  368.3 25.9 %reduce-scatter.14.cloned.1.call-done = f32[1024,64]{0,1:T(8,128)} async-done(((f32[1024,256]{0,1:T(8,128)}), f32[1024,64]{0,1:T(8,128)}) %reduce-scatter.14.cloned.1.call-update) | async-done | bytes 262160 | tf_op jit(solution)/shard_map/reduce_scatter | solution.py:30
  (33 shorter events, 3.7 us)
Async XLA Ops:
  6.5 29.4 %reduce-scatter.6.cloned.1.call-start = ((), (), s32[]{:S(2)}) async-start(), calls=%async_computation.5 | async-start | bytes 1310720 | tf_op jit(solution)/shard_map/reduce_scatter | solution.py:30
  10.0 83.8 %all-reduce.5.cloned.1.call-start = ((), (), s32[]{:S(2)}) async-start(), calls=%async_computation.6 | async-start | bytes 2097152 | tf_op jit(solution)/shard_map/psum | solution.py:27
  52.6 41.2 %copy-start = (bf16[5,1024,256]{2,1,0:T(8,128)(2,1)S(1)}, bf16[5,1024,256]{2,1,0:T(8,128)(2,1)}, u32[]{:S(2)}) copy-start(bf16[5,1024,256]{2,1,0:T(8,128)(2,1)} %param.5) | copy-start | bytes 7864324
  56.1 67.4 %reduce-scatter.8.cloned.1.call-start = ((), (), s32[]{:S(2)}) async-start(), calls=%async_computation.7 | async-start | bytes 1310720 | tf_op jit(solution)/shard_map/reduce_scatter | solution.py:30
  97.5 86.7 %all-reduce.7.cloned.1.call-start = ((), (), s32[]{:S(2)}) async-start(), calls=%async_computation.8 | async-start | bytes 2097152 | tf_op jit(solution)/shard_map/psum | solution.py:27
  140.0 0.8 copy-start.4
  146.5 67.4 %reduce-scatter.10.cloned.1.call-start = ((), (), s32[]{:S(2)}) async-start(), calls=%async_computation.9 | async-start | bytes 1310720 | tf_op jit(solution)/shard_map/reduce_scatter | solution.py:30
  187.9 86.8 %all-reduce.9.cloned.1.call-start = ((), (), s32[]{:S(2)}) async-start(), calls=%async_computation.10 | async-start | bytes 2097152 | tf_op jit(solution)/shard_map/psum | solution.py:27
  213.9 19.8 %copy-start.3 = (f32[256,1024]{0,1:T(8,128)S(1)}, f32[256,1024]{0,1:T(8,128)}, u32[]{:S(2)}) copy-start(f32[256,1024]{0,1:T(8,128)} %fusion.14) | copy-start | bytes 3145732
  230.5 0.8 copy-start.5
  237.0 67.4 %reduce-scatter.12.cloned.1.call-start = ((), (), s32[]{:S(2)}) async-start(), calls=%async_computation.11 | async-start | bytes 1310720 | tf_op jit(solution)/shard_map/reduce_scatter | solution.py:30
  278.4 86.2 %all-reduce.11.cloned.1.call-start = ((), (), s32[]{:S(2)}) async-start(), calls=%async_computation.12 | async-start | bytes 2097152 | tf_op jit(solution)/shard_map/psum | solution.py:27
  278.5 3.6 copy-start.6
  304.4 19.1 %copy-start.1 = (f32[256,1024]{0,1:T(8,128)S(1)}, f32[256,1024]{0,1:T(8,128)}, u32[]{:S(2)}) copy-start(f32[256,1024]{0,1:T(8,128)} %fusion.6) | copy-start | bytes 3145732
  304.4 19.1 %copy-start.2 = (f32[256,1024]{0,1:T(8,128)S(1)}, f32[256,1024]{0,1:T(8,128)}, u32[]{:S(2)}) copy-start(f32[256,1024]{0,1:T(8,128)} %fusion.4) | copy-start | bytes 3145732
  326.8 67.4 %reduce-scatter.14.cloned.1.call-start = ((), (), s32[]{:S(2)}) async-start(), calls=%async_computation.13 | async-start | bytes 1310720 | tf_op jit(solution)/shard_map/reduce_scatter | solution.py:30
Sparse Core Ops, SparseCore 0:
  10.1 25.8 reduce-scatter.5
  56.2 37.5 all-reduce.4
  97.6 25.7 reduce-scatter.7
  146.6 37.5 all-reduce.6
  188.0 25.7 reduce-scatter.9
  237.1 37.5 all-reduce.8
  278.6 25.7 reduce-scatter.11
  327.0 37.5 all-reduce.10
  368.4 25.7 reduce-scatter.13
where the time goes:
time: 407 us; the launch traced here: 402 us
  waiting for transfers between devices  270 us (66%)
  blocking collectives  59.8 us (15%)
  matrix products  49 us (12%)
  between operations  13.3 us (3%)
  other arithmetic  8.36 us (2%)
    psum x4, waiting for transfers between devices, per_device(): residual = residual - lax.psum(partial_value, 'col')  151 us
    reduce_scatter x5, waiting for transfers between devices, per_device(): lax.psum_scatter(term, 'row', scatter_dimension=1, tiled=True)  119 us
    all_gather x4, blocking collectives, per_device(): current = lax.all_gather(share, 'row', axis=1, tiled=True)  59.8 us
    dot_general x10, matrix products, per_device(): jnp.dot(factor_blocks[pair_index(block_row, column_index)], solved[column...  30.9 us
    dot_general x5, matrix products, per_device(): jnp.dot(inverse_blocks[block_row], residual_bf, preferred_element_type=jn...  18.1 us
  transfers between devices with their start and end apart: 9, of which 9 were waited for; matrix products, arithmetic and copies ran while one was open for 3% of the time, Pallas kernels for 0%

commit v1 on v0

v1 whole, which is shorter than its diff:
```python
import functools

import jax
import jax.numpy as jnp
from jax import lax
from jax.experimental import pallas as pl
from jax.experimental.pallas import tpu as pltpu
from jax.sharding import PartitionSpec as P

MESH = pl.DeviceIdType.MESH
CHAINS = 2
PIECES = 4


def pair_index(block_row, column_index):
    return block_row * (block_row - 1) // 2 + column_index


def kernel(
    factor_hbm, inverse_hbm, right_hbm, solved,
    factor, inverse, right, partial, pair_out, pair_in, far_out, far_in, residual, line_out, line_in, cross_in,
    load_sem, col_send, col_recv, row_send, row_recv,
):
    f32, bf16 = jnp.float32, jnp.bfloat16
    steps, chains, col_rows, width = solved.shape
    rows = right.shape[1]
    half = rows // 2
    piece = col_rows // PIECES
    row_at = lax.axis_index("row")
    col_at = lax.axis_index("col")
    group_at = lax.axis_index("groups")
    core = lax.rem(col_at, 2)
    inner = jnp.logical_or(row_at == 1, row_at == 2)
    outer = jnp.logical_not(inner)

    sibling = (group_at, row_at, col_at + 1 - 2 * core)
    far = (group_at, row_at, lax.rem(col_at + 2, 4))
    beside = (group_at, row_at + 1 - 2 * lax.rem(row_at, 2), col_at)
    across = (group_at, 3 - row_at, col_at)

    loads = {}
    order = [("r", i) for i in range(steps)][:1] + [("i", 0)]
    for i in range(1, steps):
        order += [("r", i)] + [("f", pair_index(i, j)) for j in range(i)] + [("i", i)]
    sources = {"f": (factor_hbm, factor), "i": (inverse_hbm, inverse), "r": (right_hbm, right)}
    for slot, (kind, at) in enumerate(order):
        src, dst = sources[kind]
        loads[kind, at] = pltpu.make_async_copy(src.at[at], dst.at[at], load_sem.at[slot])
        loads[kind, at].start()
    waited = set()

    def loaded(kind, at):
        if (kind, at) not in waited:
            waited.add((kind, at))
            loads[kind, at].wait()

    barrier = pltpu.get_barrier_semaphore()
    for peer in (sibling, far, beside):
        pl.semaphore_signal(barrier, inc=1, device_id=peer, device_id_type=MESH)

    @pl.when(inner)
    def _():
        pl.semaphore_signal(barrier, inc=1, device_id=across, device_id_type=MESH)
        pl.semaphore_wait(barrier, 4)

    @pl.when(outer)
    def _():
        pl.semaphore_wait(barrier, 3)

    def remote(src, dst, send, recv, peer):
        return pltpu.make_async_remote_copy(
            src_ref=src, dst_ref=dst, send_sem=send, recv_sem=recv, device_id=peer, device_id_type=MESH
        )

    mine = pl.ds(pl.multiple_of(core * half, half), half)
    other = pl.ds(pl.multiple_of((1 - core) * half, half), half)

    def dot(a, b):
        return jnp.dot(a, b, preferred_element_type=f32)

    def chain(a):
        lanes = slice(a * width, (a + 1) * width)
        for i in range(steps):
            if i > 0:
                to_pair = remote(pair_out.at[i - 1, a], pair_in.at[i - 1, a], col_send.at[i - 1, a, 0], col_recv.at[i - 1, a, 0], sibling)
                to_far = remote(far_out.at[i - 1, a], far_in.at[i - 1, a], col_send.at[i - 1, a, 1], col_recv.at[i - 1, a, 1], far)
                back = remote(residual.at[i, a, mine], residual.at[i, a, mine], col_send.at[i - 1, a, 2], col_recv.at[i - 1, a, 2], sibling)
                at = pair_index(i, i - 1)
                loaded("f", at)
                value = dot(factor[at, other, :], solved[i - 1, a])
                if i > 1:
                    value = value + partial[a, other, :]
                pair_out[i - 1, a] = value.astype(bf16)
                to_pair.start()
                value = dot(factor[at, mine, :], solved[i - 1, a])
                if i > 1:
                    value = value + partial[a, mine, :]
                partial[a, mine, :] = value
                yield
                to_pair.wait_recv()
                far_out[i - 1, a] = (partial[a, mine, :] + pair_in[i - 1, a].astype(f32)).astype(bf16)
                to_far.start()
                yield
                to_far.wait_recv()
                loaded("r", i)
                total = far_out[i - 1, a].astype(f32) + far_in[i - 1, a].astype(f32)
                residual[i, a, mine, :] = (right[i, mine, lanes].astype(f32) - total).astype(bf16)
                back.start()
                yield
                back.wait_recv()
            else:
                loaded("r", 0)
                residual[0, a] = right[0, :, lanes]
            loaded("i", i)
            spans = [pl.ds(k * piece, piece) for k in range(PIECES)]
            first = [remote(line_out.at[i, a, s], line_in.at[i, a, s], row_send.at[i, a, 0, k], row_recv.at[i, a, 0, k], beside) for k, s in enumerate(spans)]
            cross = [remote(line_out.at[i, a, s], cross_in.at[i, a, s], row_send.at[i, a, 1, k], row_recv.at[i, a, 1, k], across) for k, s in enumerate(spans)]
            last = [remote(solved.at[i, a, s], solved.at[i, a, s], row_send.at[i, a, 2, k], row_recv.at[i, a, 2, k], beside) for k, s in enumerate(spans)]
            for k, s in enumerate(spans):
                term = dot(inverse[i, s, :], residual[i, a])

                @pl.when(outer)
                def _():
                    line_out[i, a, s, :] = term.astype(bf16)
                    first[k].start()

                @pl.when(inner)
                def _():
                    first[k].wait_recv()
                    line_out[i, a, s, :] = (term + line_in[i, a, s, :].astype(f32)).astype(bf16)
                    cross[k].start()

            if i > 0 and i + 1 < steps:
                for j in range(i):
                    loaded("f", pair_index(i + 1, j))

                def ahead(t, carry):
                    tile = pl.ds(pl.multiple_of(t * piece, piece), piece)
                    value = dot(factor[pair_index(i + 1, 0), tile, :], solved[0, a])
                    for j in range(1, i):
                        value = value + dot(factor[pair_index(i + 1, j), tile, :], solved[j, a])
                    partial[a, tile, :] = value
                    return carry

                lax.fori_loop(0, rows // piece, ahead, 0)
            yield

            @pl.when(inner)
            def _():
                for k, s in enumerate(spans):
                    cross[k].wait_recv()
                    value = line_out[i, a, s, :].astype(f32) + cross_in[i, a, s, :].astype(f32)
                    solved[i, a, s, :] = value.astype(bf16)
                    last[k].start()

            yield

            @pl.when(outer)
            def _():
                for k in range(PIECES):
                    last[k].wait_recv()
                    first[k].wait_send()

            @pl.when(inner)
            def _():
                for k in range(PIECES):
                    cross[k].wait_send()
                    last[k].wait_send()

            if i > 0:
                to_pair.wait_send()
                to_far.wait_send()
                back.wait_send()

    running = [chain(a) for a in range(chains)]
    turn = 0
    while running:
        active = [g for a, g in enumerate(running) if a * 3 <= turn]
        for g in active:
            try:
                next(g)
            except StopIteration:
                running = [other_g for other_g in running if other_g is not g]
        turn += 1


def line_solve(factor_blocks, inverse_blocks, right_sides):
    steps, rows, angles = right_sides.shape
    pairs = factor_blocks.shape[0]
    col_rows = inverse_blocks.shape[1]
    width = angles // CHAINS
    half = rows // 2
    bf16 = jnp.bfloat16
    sweeps = steps - 1
    wide = (steps, CHAINS, col_rows, width)
    dma = pltpu.SemaphoreType.DMA
    solved = pl.pallas_call(
        kernel,
        out_shape=jax.ShapeDtypeStruct(wide, bf16),
        in_specs=[pl.BlockSpec(memory_space=pl.ANY)] * 3,
        out_specs=pl.BlockSpec(memory_space=pltpu.VMEM),
        scratch_shapes=[
            pltpu.VMEM(factor_blocks.shape, bf16),
            pltpu.VMEM(inverse_blocks.shape, bf16),
            pltpu.VMEM(right_sides.shape, bf16),
            pltpu.VMEM((CHAINS, rows, width), jnp.float32),
            pltpu.VMEM((sweeps, CHAINS, half, width), bf16),
            pltpu.VMEM((sweeps, CHAINS, half, width), bf16),
            pltpu.VMEM((sweeps, CHAINS, half, width), bf16),
            pltpu.VMEM((sweeps, CHAINS, half, width), bf16),
            pltpu.VMEM((steps, CHAINS, rows, width), bf16),
            pltpu.VMEM(wide, bf16),
            pltpu.VMEM(wide, bf16),
            pltpu.VMEM(wide, bf16),
            dma((pairs + 2 * steps,)),
            dma((sweeps, CHAINS, 3)),
            dma((sweeps, CHAINS, 3)),
            dma((steps, CHAINS, 3, PIECES)),
            dma((steps, CHAINS, 3, PIECES)),
        ],
        compiler_params=pltpu.CompilerParams(
            collective_id=0, has_side_effects=True, vmem_limit_bytes=67043328
        ),
    )(factor_blocks, inverse_blocks, right_sides)
    share = angles // lax.axis_size("row")
    start = lax.axis_index("row") * share
    held = lax.dynamic_index_in_dim(solved, start // width, axis=1, keepdims=False)
    return lax.dynamic_slice_in_dim(held, lax.rem(start, width), share, axis=2)


def plain_solve(factor_blocks, inverse_blocks, right_sides):
    steps_total = right_sides.shape[0]
    solved = []
    outputs = []
    for block_row in range(steps_total):
        residual = right_sides[block_row].astype(jnp.float32)
        if block_row > 0:
            partial_value = jnp.zeros(residual.shape, jnp.float32)
            for column_index in range(block_row):
                partial_value = partial_value + jnp.dot(
                    factor_blocks[pair_index(block_row, column_index)],
                    solved[column_index],
                    preferred_element_type=jnp.float32,
                )
            residual = residual - lax.psum(partial_value, "col")
        residual_bf = residual.astype(jnp.bfloat16)
        term = jnp.dot(inverse_blocks[block_row], residual_bf, preferred_element_type=jnp.float32)
        share = lax.psum_scatter(term, "row", scatter_dimension=1, tiled=True).astype(jnp.bfloat16)
        outputs.append(share)
        if block_row + 1 < steps_total:
            solved.append(lax.all_gather(share, "row", axis=1, tiled=True))
    return jnp.stack(outputs, axis=0)


def solution(mesh):
    placed = (P("groups", "row", "col"), P("groups", "col", "row"), P("groups", "row", None))
    per_device = line_solve if mesh.shape["row"] == 4 and mesh.shape["col"] == 4 else plain_solve
    return jax.shard_map(
        per_device, mesh=mesh, in_specs=placed, out_specs=P("groups", "col", "row"), check_vma=False
    )
```

time: 407 us -> 150 us (0.37)
  the two profiles are of different devices: /device:TPU:26 before, /device:TPU:0 now
where the time goes in v1:
time: 150 us
  Pallas kernels  147 us (98%)
  local copies, waits for them, and re-layouts  3.04 us (2%)
    pallas_call x1, Pallas kernels, line_solve(): pl.pallas_call(kernel, out_shape=jax.ShapeDtypeStruct(wide, bf16), in_spe...  147 us
    dynamic_slice x2, local copies, waits for them, and re-layouts, line_solve(): return lax.dynamic_slice_in_dim(held, lax.rem(start, width), share, axis=2)  3.04 us

profile of v1, /device:TPU:0, one launch (start us, length us, event | category | flops | bytes accessed | tf_op | source)
XLA Modules:
  0.0 150.2 jit_solution(15873312533449141677)
XLA Ops:
  0.0 147.2 %shard_map.37 = bf16[5,2,1024,128]{3,2,1,0:T(8,128)(2,1)} custom-call(bf16[10,1024,1024]{2,1,0:T(8,128)(2,1)} %factor_hbm.1, bf16[5,1024,1024]{2,1,0:T(8,128)(2,1)} %inverse_hbm.1, bf16[5,1024,256]{2,1,0:T(8,128)(2,1)} %right_hbm.1), custom_call_target="tpu_custom_call" | custom-call | tf_op jit(solution)/shard_map/pallas_call | solution.py:197
  147.2 1.7 %constant_dynamic-slice_fusion = bf16[5,1,1024,64]{3,2,1,0:T(8,128)(2,1)S(1)} fusion(bf16[5,2,1024,128]{3,2,1,0:T(8,128)(2,1)} %shard_map.37, s32[]{:T(128)S(6)} %select_n.18, s32[]{:T(128)S(6)} %select_n.20), kind=kLoop, calls=%fused_computation | loop fusion | bytes 1310728 | tf_op jit(solution)/shard_map/dynamic_slice | solution.py:228
  148.9 1.3 copy.4

commit v2 on v1

--- a/solution.py
+++ b/solution.py
@@ -10,6 +10,7 @@
 MESH = pl.DeviceIdType.MESH
 CHAINS = 2
 PIECES = 4
+STAGGER = 1
 
 
 def pair_index(block_row, column_index):
@@ -32,6 +33,7 @@
     core = lax.rem(col_at, 2)
     inner = jnp.logical_or(row_at == 1, row_at == 2)
     outer = jnp.logical_not(inner)
+    owns = [row_at * chains // 4 == a for a in range(chains)]
 
     sibling = (group_at, row_at, col_at + 1 - 2 * core)
     far = (group_at, row_at, lax.rem(col_at + 2, 4))
@@ -112,6 +114,9 @@
                 loaded("r", 0)
                 residual[0, a] = right[0, :, lanes]
             loaded("i", i)
+            final = i + 1 == steps
+            takes = owns[a] if final else True
+            gives = jnp.logical_not(owns[a]) if final else True
             spans = [pl.ds(k * piece, piece) for k in range(PIECES)]
             first = [remote(line_out.at[i, a, s], line_in.at[i, a, s], row_send.at[i, a, 0, k], row_recv.at[i, a, 0, k], beside) for k, s in enumerate(spans)]
             cross = [remote(line_out.at[i, a, s], cross_in.at[i, a, s], row_send.at[i, a, 1, k], row_recv.at[i, a, 1, k], across) for k, s in enumerate(spans)]
@@ -128,6 +133,9 @@
                 def _():
                     first[k].wait_recv()
                     line_out[i, a, s, :] = (term + line_in[i, a, s, :].astype(f32)).astype(bf16)
+
+                @pl.when(jnp.logical_and(inner, gives))
+                def _():
                     cross[k].start()
 
             if i > 0 and i + 1 < steps:
@@ -145,7 +153,7 @@
                 lax.fori_loop(0, rows // piece, ahead, 0)
             yield
 
-            @pl.when(inner)
+            @pl.when(jnp.logical_and(inner, takes))
             def _():
                 for k, s in enumerate(spans):
                     cross[k].wait_recv()
@@ -155,16 +163,24 @@
 
             yield
 
+            @pl.when(jnp.logical_and(outer, takes))
+            def _():
+                for k in range(PIECES):
+                    last[k].wait_recv()
+
             @pl.when(outer)
             def _():
                 for k in range(PIECES):
-                    last[k].wait_recv()
                     first[k].wait_send()
 
-            @pl.when(inner)
+            @pl.when(jnp.logical_and(inner, gives))
             def _():
                 for k in range(PIECES):
                     cross[k].wait_send()
+
+            @pl.when(jnp.logical_and(inner, takes))
+            def _():
+                for k in range(PIECES):
                     last[k].wait_send()
 
             if i > 0:
@@ -175,7 +191,7 @@
     running = [chain(a) for a in range(chains)]
     turn = 0
     while running:
-        active = [g for a, g in enumerate(running) if a * 3 <= turn]
+        active = [g for a, g in enumerate(running) if a * STAGGER <= turn]
         for g in active:
             try:
                 next(g)

time: 150 us -> 136 us (0.907)
  the two profiles are of different devices: /device:TPU:0 before, /device:TPU:26 now
where the time goes in v2:
time: 136 us
  Pallas kernels  133 us (98%)
  local copies, waits for them, and re-layouts  3.04 us (2%)
    pallas_call x1, Pallas kernels, line_solve(): pl.pallas_call(kernel, out_shape=jax.ShapeDtypeStruct(wide, bf16), in_spe...  133 us
    dynamic_slice x2, local copies, waits for them, and re-layouts, line_solve(): return lax.dynamic_slice_in_dim(held, lax.rem(start, width), share, axis=2)  3.04 us

profile of v2, /device:TPU:26, one launch (start us, length us, event | category | flops | bytes accessed | tf_op | source)
XLA Modules:
  0.0 136.3 jit_solution(8197540777103053289)
XLA Ops:
  0.0 133.3 %shard_map.37 = bf16[5,2,1024,128]{3,2,1,0:T(8,128)(2,1)} custom-call(bf16[10,1024,1024]{2,1,0:T(8,128)(2,1)} %factor_hbm.1, bf16[5,1024,1024]{2,1,0:T(8,128)(2,1)} %inverse_hbm.1, bf16[5,1024,256]{2,1,0:T(8,128)(2,1)} %right_hbm.1), custom_call_target="tpu_custom_call" | custom-call | tf_op jit(solution)/shard_map/pallas_call | solution.py:213
  133.3 1.7 %constant_dynamic-slice_fusion = bf16[5,1,1024,64]{3,2,1,0:T(8,128)(2,1)S(1)} fusion(bf16[5,2,1024,128]{3,2,1,0:T(8,128)(2,1)} %shard_map.37, s32[]{:T(128)S(6)} %select_n.18, s32[]{:T(128)S(6)} %select_n.20), kind=kLoop, calls=%fused_computation | loop fusion | bytes 1310728 | tf_op jit(solution)/shard_map/dynamic_slice | solution.py:244
  135.0 1.3 copy.4

commit v3 on v2

--- a/solution.py
+++ b/solution.py
@@ -131,8 +131,17 @@
 
                 @pl.when(inner)
                 def _():
+                    partial[a, s, :] = term
+
+            yield
+
+            for k, s in enumerate(spans):
+
+                @pl.when(inner)
+                def _():
                     first[k].wait_recv()
-                    line_out[i, a, s, :] = (term + line_in[i, a, s, :].astype(f32)).astype(bf16)
+                    value = partial[a, s, :] + line_in[i, a, s, :].astype(f32)
+                    line_out[i, a, s, :] = value.astype(bf16)
 
                 @pl.when(jnp.logical_and(inner, gives))
                 def _():

time: 136 us -> 139 us (1.022)
  Pallas kernels: 133 us -> 135 us
    pallas_call x1, Pallas kernels: 133 us -> 135 us  [line_solve(): pl.pallas_call(kernel, out_shape=jax.ShapeDtypeStruct(wide, bf16), in_spe...]
where the time goes in v3:
time: 139 us; the launch traced here: 138 us
  Pallas kernels  135 us (97%)
  local copies, waits for them, and re-layouts  3.04 us (2%)
    pallas_call x1, Pallas kernels, line_solve(): pl.pallas_call(kernel, out_shape=jax.ShapeDtypeStruct(wide, bf16), in_spe...  135 us
    dynamic_slice x2, local copies, waits for them, and re-layouts, line_solve(): return lax.dynamic_slice_in_dim(held, lax.rem(start, width), share, axis=2)  3.04 us

profile of v3, /device:TPU:26, one launch (start us, length us, event | category | flops | bytes accessed | tf_op | source)
XLA Modules:
  0.0 138.4 jit_solution(5588714712666575123)
XLA Ops:
  0.0 135.3 %shard_map.37 = bf16[5,2,1024,128]{3,2,1,0:T(8,128)(2,1)} custom-call(bf16[10,1024,1024]{2,1,0:T(8,128)(2,1)} %factor_hbm.1, bf16[5,1024,1024]{2,1,0:T(8,128)(2,1)} %inverse_hbm.1, bf16[5,1024,256]{2,1,0:T(8,128)(2,1)} %right_hbm.1), custom_call_target="tpu_custom_call" | custom-call | tf_op jit(solution)/shard_map/pallas_call | solution.py:222
  135.3 1.7 %constant_dynamic-slice_fusion = bf16[5,1,1024,64]{3,2,1,0:T(8,128)(2,1)S(1)} fusion(bf16[5,2,1024,128]{3,2,1,0:T(8,128)(2,1)} %shard_map.37, s32[]{:T(128)S(6)} %select_n.18, s32[]{:T(128)S(6)} %select_n.20), kind=kLoop, calls=%fused_computation | loop fusion | bytes 1310728 | tf_op jit(solution)/shard_map/dynamic_slice | solution.py:253
  137.1 1.3 copy.4
